TPU v7x, 768 devices: a whole 4x8x12 slice. The times are simulated.
768 devices in a mesh: energy: 24 (over x, z_lo, core), atom: 32 (over y, z_hi).
Axes of the slice: x: 4, y: 8, z: 12 (z_hi: 4, z_lo: 3; z = z_hi * 3 + z_lo), core: 2. Of those that a mesh axis runs over, the one named last changes fastest.
Arguments:
- green: float32 [2, 48, 64, 128, 128], P(None, 'energy', 'atom'), may hold values from -6 to 6
- coupling: float32 [64, 6, 128, 128], P('atom'), may hold values from -0.5 to 0.5
- phonon: float32 [64, 6, 4], P('atom'), may hold values from 0.2 to 2
- neighbours: int32 [64, 6], P('atom'), may hold values from 0 to 63, as said below
Outputs:
- self_energy: float32 [2, 48, 64, 128, 128], P(None, 'energy', 'atom')
- rates: float32 [64, 128], P('atom')
Inputs may be any that keep to these rules, and one draw needn't show every extreme that they name: `neighbours`: each entry lies within 2 of its row's index and within 0 to 63; offsets +2 and -2 both occur.
All inputs are finite; a program needn't handle non-finite values.
Results may differ from a plain program's by a relative error of at most 0.000071.
Values sent between devices are 32-bit elements; how exact they have to be, the bound alone decides.
A program may use at most 32 MiB of HBM per device.

v0:
```python
import jax
import jax.numpy as jnp
from jax import lax
from jax.sharding import PartitionSpec as P


def extended(shard, sides, width):
    for axis, dim in sides:
        devices, length = (lax.axis_size(axis), shard.shape[dim])
        up = [(i, (i + 1) % devices) for i in range(devices - 1)]
        down = [(j, i) for i, j in up]
        last = lax.slice_in_dim(shard, length - width, length, axis=dim)
        leading = lax.slice_in_dim(shard, 0, width, axis=dim)
        before = lax.ppermute(last, axis, up)
        after = lax.ppermute(leading, axis, down)
        shard = jnp.concatenate([before, shard, after], axis=dim)
    return shard


def per_device(green, coupling, phonon, neighbours):
    highest = lax.Precision.HIGHEST
    shifts = (-2, -1, 1, 2)
    e_local = green.shape[1]
    a_local = green.shape[2]
    widened = extended(green, (("energy", 1), ("atom", 2)), 2)
    first_atom = lax.axis_index("atom") * a_local
    sigma = jnp.zeros_like(green)
    for slot in range(coupling.shape[1]):
        rows = neighbours[:, slot] - first_atom + 2
        near = jnp.take(widened, rows, axis=2)
        mixed = jnp.zeros_like(green)
        for step in range(4):
            start = 2 + shifts[step]
            factor = phonon[:, slot, step][None, None, :, None, None]
            mixed = mixed + factor * near[:, start : start + e_local]
        mats = coupling[:, slot]
        inner = jnp.einsum("aik,ceakl->ceail", mats, mixed, precision=highest)
        sigma = sigma + jnp.einsum("ceail,aml->ceaim", inner, mats, precision=highest)
    partial_rate = jnp.einsum("eail,eali->ai", sigma[0], green[0], precision=highest) - jnp.einsum(
        "eail,eali->ai", sigma[1], green[1], precision=highest
    )
    total_rate = lax.psum(partial_rate, "energy")
    points = e_local * lax.axis_size("energy")
    return (sigma, total_rate / (4.0 * points))


def solution(mesh):
    return jax.shard_map(
        per_device,
        mesh=mesh,
        in_specs=(
            P(None, "energy", "atom", None, None),
            P("atom", None, None, None),
            P("atom", None, None),
            P("atom", None),
        ),
        out_specs=(P(None, "energy", "atom", None, None), P("atom", None)),
        check_vma=False,
    )
```

profile of v0, /device:TPU:246, one launch (start us, length us, event | category | flops | bytes accessed | tf_op | source)
XLA Modules:
  0.0 222.6 jit_solution(12926533919904347646)
XLA Ops:
  0.6 1.9 collective-permute-start
  2.6 7.0 %collective-permute-start.1 = (f32[2,2,2,128,128]{4,3,2,1,0:T(8,128)}, f32[2,2,2,128,128]{4,3,2,1,0:T(8,128)S(1)}, u32[]{:S(2)}, u32[]{:S(2)}) collective-permute-start(f32[2,2,2,128,128]{4,3,2,1,0:T(8,128)} %param.6), channel_id=1, source_target_pairs={{32,0},{64,32},{96,64},{128,96},{160,128},{192,160},{224,192},{256... | collective-permute-start | bytes 1572872 | tf_op jit(solution)/shard_map/ppermute | solution.py:15
  9.6 1.2 add_reduce_fusion
  10.8 5.0 %collective-permute-done = f32[2,2,2,128,128]{4,3,2,1,0:T(8,128)S(1)} collective-permute-done((f32[2,2,2,128,128]{4,3,2,1,0:T(8,128)}, f32[2,2,2,128,128]{4,3,2,1,0:T(8,128)S(1)}, u32[]{:S(2)}, u32[]{:S(2)}) %collective-permute-start) | collective-permute-done | bytes 524320 | tf_op jit(solution)/shard_map/ppermute | solution.py:14
  15.9 1.1 constant_dynamic-update-slice_fusion.1
  16.9 1.2 collective-permute-done.1
  18.2 1.9 collective-permute-start.3
  20.1 42.7 %collective-permute-start.2 = (f32[2,6,2,128,128]{4,3,2,1,0:T(8,128)S(1)}, f32[2,6,2,128,128]{4,3,2,1,0:T(8,128)S(1)}, u32[]{:S(2)}, u32[]{:S(2)}) collective-permute-start(f32[2,6,2,128,128]{4,3,2,1,0:T(8,128)S(1)} %constant_dynamic-update-slice_fusion), channel_id=1, source_target_pairs={{0,1},{1,2},{2,3},{3,4},{4,5},{5,6},{6,7},{7,8},{8,9},{9,10},{10,1... | collective-permute-start | bytes 4718600 | tf_op jit(solution)/shard_map/ppermute | solution.py:14
  63.4 61.6 %collective-permute-done.3 = f32[2,6,2,128,128]{4,3,2,1,0:T(8,128)S(1)} collective-permute-done((f32[2,6,2,128,128]{4,3,2,1,0:T(8,128)S(1)}, f32[2,6,2,128,128]{4,3,2,1,0:T(8,128)S(1)}, u32[]{:S(2)}, u32[]{:S(2)}) %collective-permute-start.3) | collective-permute-done | bytes 1572896 | tf_op jit(solution)/shard_map/ppermute | solution.py:15
  124.9 2.4 %pad_maximum_fusion = f32[2,6,6,128,128]{4,3,2,1,0:T(8,128)} fusion(f32[2,6,2,128,128]{4,3,2,1,0:T(8,128)S(1)} %collective-permute-done.3, f32[2,6,2,128,128]{4,3,2,1,0:T(8,128)S(1)} %constant_dynamic-update-slice_fusion, f32[2,6,2,128,128]{4,3,2,1,0:T(8,128)S(1)} %collective-permute-done.2), kind=kLoop, calls=%fused_computation.6 | loop fusion | flops 2359296 | bytes 9437184 | tf_op jit(solution)/shard_map/concatenate | solution.py:16
  127.4 3.0 %gather_fusion = f32[2,2,6,128,128]{4,3,2,1,0:T(8,128)S(1)} fusion(f32[2,6,6,128,128]{4,3,2,1,0:T(8,128)} %pad_maximum_fusion, s32[1024]{0:T(1024)S(1)} %pad_clamp_fusion.5), kind=kCustom, calls=%fused_computation.clone | custom fusion | bytes 3145736 | tf_op jit(solution)/shard_map/jit(_take)/gather | solution.py:30
  130.6 1.7 convolution_bitcast_fusion.5
  132.3 2.3 %fusion.73 = f32[2,2,2,128,128]{4,3,2,1,0:T(8,128)} fusion(f32[2,2,2,128,128]{4,3,1,0,2:T(8,128)S(1)} %convolution_bitcast_fusion.5, f32[2,6,128,128]{3,2,1,0:T(8,128)} %param.7), kind=kOutput, calls=%fused_computation.107 | convolution fusion | flops 201326592 | bytes 1179648 | tf_op jit(solution)/shard_map/ceail,aml->ceaim/dot_general | solution.py:38
  134.6 4.2 %gather_fusion.1 = f32[2,2,6,128,128]{4,3,2,1,0:T(8,128)} fusion(f32[2,6,6,128,128]{4,3,2,1,0:T(8,128)} %pad_maximum_fusion, s32[1024]{0:T(1024)S(1)} %pad_clamp_fusion.4), kind=kCustom, calls=%fused_computation.1.clone | custom fusion | bytes 3145736 | tf_op jit(solution)/shard_map/jit(_take)/gather | solution.py:30
  138.8 4.1 %gather_fusion.2 = f32[2,2,6,128,128]{4,3,2,1,0:T(8,128)} fusion(f32[2,6,6,128,128]{4,3,2,1,0:T(8,128)} %pad_maximum_fusion, s32[1024]{0:T(1024)S(1)} %pad_clamp_fusion.3), kind=kCustom, calls=%fused_computation.2.clone | custom fusion | bytes 3145736 | tf_op jit(solution)/shard_map/jit(_take)/gather | solution.py:30
  142.9 4.2 %gather_fusion.3 = f32[2,2,6,128,128]{4,3,2,1,0:T(8,128)} fusion(f32[2,6,6,128,128]{4,3,2,1,0:T(8,128)} %pad_maximum_fusion, s32[1024]{0:T(1024)S(1)} %pad_clamp_fusion.2), kind=kCustom, calls=%fused_computation.3.clone | custom fusion | bytes 3145736 | tf_op jit(solution)/shard_map/jit(_take)/gather | solution.py:30
  147.1 3.0 %gather_fusion.4 = f32[2,2,6,128,128]{4,3,2,1,0:T(8,128)S(1)} fusion(f32[2,6,6,128,128]{4,3,2,1,0:T(8,128)} %pad_maximum_fusion, s32[1024]{0:T(1024)S(1)} %pad_clamp_fusion.1), kind=kCustom, calls=%fused_computation.4.clone | custom fusion | bytes 3145736 | tf_op jit(solution)/shard_map/jit(_take)/gather | solution.py:30
  150.1 3.0 %gather_fusion.5 = f32[2,2,6,128,128]{4,3,2,1,0:T(8,128)S(1)} fusion(f32[2,6,6,128,128]{4,3,2,1,0:T(8,128)} %pad_maximum_fusion, s32[1024]{0:T(1024)S(1)} %pad_clamp_fusion), kind=kCustom, calls=%fused_computation.5.clone | custom fusion | bytes 3145736 | tf_op jit(solution)/shard_map/jit(_take)/gather | solution.py:30
  153.1 1.7 select_bitcast_fusion.4
  154.9 0.8 convolution_bitcast_fusion.4
  155.7 0.6 convolution_add_fusion.4
  156.5 0.8 convolution_bitcast_fusion.3
  157.3 0.6 convolution_add_fusion.3
  158.2 0.8 convolution_bitcast_fusion.2
  159.0 0.6 convolution_add_fusion.2
  159.8 0.8 convolution_bitcast_fusion.1
  160.6 0.6 convolution_add_fusion.1
  161.5 0.8 convolution_bitcast_fusion
  162.3 0.6 fusion
  162.9 0.8 copy.19
  164.2 57.9 %psum.7 = f32[2,128]{1,0:T(2,128)S(1)} all-reduce(f32[2,128]{1,0:T(2,128)S(1)} %sub.42), channel_id=1, replica_groups=mesh['energy'=24,'atom'=32] {'energy'}, use_global_device_ids=true, to_apply=%region_0.0 | all-reduce | flops 256 | bytes 2048 | tf_op jit(solution)/shard_map/psum | solution.py:42
  222.1 0.6 broadcast_multiply_fusion
  (39 shorter events, 2.2 us)
Async XLA Ops:
  0.6 15.2 %collective-permute-start = (f32[2,2,2,128,128]{4,3,2,1,0:T(8,128)}, f32[2,2,2,128,128]{4,3,2,1,0:T(8,128)S(1)}, u32[]{:S(2)}, u32[]{:S(2)}) collective-permute-start(f32[2,2,2,128,128]{4,3,2,1,0:T(8,128)} %param.6), channel_id=1, source_target_pairs={{0,32},{32,64},{64,96},{96,128},{128,160},{160,192},{192,224},{224... | collective-permute-start | bytes 1572872 | tf_op jit(solution)/shard_map/ppermute | solution.py:14
  2.6 15.6 %collective-permute-start.1 = (f32[2,2,2,128,128]{4,3,2,1,0:T(8,128)}, f32[2,2,2,128,128]{4,3,2,1,0:T(8,128)S(1)}, u32[]{:S(2)}, u32[]{:S(2)}) collective-permute-start(f32[2,2,2,128,128]{4,3,2,1,0:T(8,128)} %param.6), channel_id=1, source_target_pairs={{32,0},{64,32},{96,64},{128,96},{160,128},{192,160},{224,192},{256... | collective-permute-start | bytes 1572872 | tf_op jit(solution)/shard_map/ppermute | solution.py:15
  10.8 52.1 %copy-start.5 = (f32[2,6,4]{1,2,0:T(4,128)S(1)}, f32[2,6,4]{1,2,0:T(4,128)}, u32[]{:S(2)}) copy-start(f32[2,6,4]{1,2,0:T(4,128)} %param.8) | copy-start | bytes 580
  18.2 106.7 %collective-permute-start.3 = (f32[2,6,2,128,128]{4,3,2,1,0:T(8,128)S(1)}, f32[2,6,2,128,128]{4,3,2,1,0:T(8,128)S(1)}, u32[]{:S(2)}, u32[]{:S(2)}) collective-permute-start(f32[2,6,2,128,128]{4,3,2,1,0:T(8,128)S(1)} %constant_dynamic-update-slice_fusion), channel_id=1, source_target_pairs={{1,0},{2,1},{3,2},{4,3},{5,4},{6,5},{7,6},{8,7},{9,8},{10,9},{11,1... | collective-permute-start | bytes 4718600 | tf_op jit(solution)/shard_map/ppermute | solution.py:15
  20.1 104.8 %collective-permute-start.2 = (f32[2,6,2,128,128]{4,3,2,1,0:T(8,128)S(1)}, f32[2,6,2,128,128]{4,3,2,1,0:T(8,128)S(1)}, u32[]{:S(2)}, u32[]{:S(2)}) collective-permute-start(f32[2,6,2,128,128]{4,3,2,1,0:T(8,128)S(1)} %constant_dynamic-update-slice_fusion), channel_id=1, source_target_pairs={{0,1},{1,2},{2,3},{3,4},{4,5},{5,6},{6,7},{7,8},{8,9},{9,10},{10,1... | collective-permute-start | bytes 4718600 | tf_op jit(solution)/shard_map/ppermute | solution.py:14
  153.1 1.8 copy-start.4
  153.1 2.6 %copy-start.3 = (f32[2,2,2,128,128]{4,3,2,1,0:T(8,128)S(1)}, f32[2,2,2,128,128]{4,3,2,1,0:T(8,128)}, u32[]{:S(2)}) copy-start(f32[2,2,2,128,128]{4,3,2,1,0:T(8,128)} %fusion.73) | copy-start | bytes 1572868
  154.9 1.4 copy-start.1
  156.5 1.4 copy-start
  162.9 1.2 copy-start.2
where the time goes:
time: 223 us
  waiting for transfers between devices  67.8 us (30%)
  blocking collectives  57.9 us (26%)
  starting transfers between devices  53.5 us (24%)
  local copies, waits for them, and re-layouts  24.2 us (11%)
  matrix products  10.9 us (5%)
  other arithmetic  7.22 us (3%)
    ppermute x2, waiting for transfers between devices, extended(): after = lax.ppermute(leading, axis, down)  62.8 us
    psum x1, blocking collectives, per_device(): total_rate = lax.psum(partial_rate, 'energy')  57.9 us
    ppermute x2, starting transfers between devices, extended(): before = lax.ppermute(last, axis, up)  44.6 us
    gather x6, local copies, waits for them, and re-layouts, per_device(): near = jnp.take(widened, rows, axis=2)  21.4 us
    ppermute x2, starting transfers between devices, extended(): after = lax.ppermute(leading, axis, down)  8.93 us
    dot_general x6, matrix products, per_device(): inner = jnp.einsum('aik,ceakl->ceail', mats, mixed, precision=highest)  5.66 us
    dot_general x6, matrix products, per_device(): jnp.einsum('ceail,aml->ceaim', inner, mats, precision=highest)  5.27 us
    ppermute x2, waiting for transfers between devices, extended(): before = lax.ppermute(last, axis, up)  5.02 us
  transfers between devices with their start and end apart: 4, of which 3 were waited for; matrix products, arithmetic and copies ran while one was open for 1% of the time, Pallas kernels for 0%

commit v1 on v0

v1 whole, which is shorter than its diff:
```python
import functools

import jax
import jax.numpy as jnp
from jax import lax
from jax.experimental import pallas as pl
from jax.experimental.pallas import tpu as pltpu
from jax.sharding import PartitionSpec as P

MESH = pl.DeviceIdType.MESH
F32 = jnp.float32
BF16 = jnp.bfloat16


def split(x):
    high = x.astype(BF16)
    low = (x - high.astype(F32)).astype(BF16)
    return high, low


def kernel(
    n_energy,
    n_atom,
    nbr,
    orb,
    nbr_ref,
    ph_ref,
    green,
    coupling,
    sigma_out,
    rates_out,
    gbuf,
    cbuf,
    cleft,
    cright,
    gs,
    tbuf,
    own,
    send_next,
    send_prev,
    from_prev,
    from_next,
    gt,
    rsrc,
    rslots,
    local_sem,
    a_send,
    a_recv,
    u_send,
    u_recv,
    r_send,
    r_recv,
    o_sem,
):
    ei = lax.axis_index("energy")
    ai = lax.axis_index("atom")
    nxt_a, prv_a = lax.rem(ai + 1, n_atom), lax.rem(ai + n_atom - 1, n_atom)
    nxt_e, prv_e = lax.rem(ei + 1, n_energy), lax.rem(ei + n_energy - 1, n_energy)

    barrier = pltpu.get_barrier_semaphore()
    pl.semaphore_signal(barrier, inc=1, device_id={"atom": nxt_a}, device_id_type=MESH)
    pl.semaphore_signal(barrier, inc=1, device_id={"atom": prv_a}, device_id_type=MESH)

    def greet(p, carry):
        peer = lax.rem(ei + p, n_energy)
        pl.semaphore_signal(barrier, inc=1, device_id={"energy": peer}, device_id_type=MESH)
        return carry

    lax.fori_loop(1, n_energy, greet, 0)

    load_c = pltpu.make_async_copy(coupling, cbuf, local_sem.at[0])
    load_g = pltpu.make_async_copy(green, gbuf.at[:, :, pl.ds(2, 2)], local_sem.at[1])
    load_c.start()
    load_g.start()

    pl.semaphore_wait(barrier, n_energy + 1)

    def atom_copy(c, e, up):
        return pltpu.make_async_remote_copy(
            src_ref=green.at[c, e],
            dst_ref=gbuf.at[c, e, pl.ds(0 if up else 4, 2)],
            send_sem=a_send.at[int(up), c * 2 + e],
            recv_sem=a_recv.at[int(up), c * 2 + e],
            device_id={"atom": nxt_a if up else prv_a},
            device_id_type=MESH,
        )

    for c in range(2):
        for e in range(2):
            atom_copy(c, e, True).start()
            atom_copy(c, e, False).start()

    def energy_copy(c, e, a, up):
        index = (c * 2 + e) * 2 + a
        return pltpu.make_async_remote_copy(
            src_ref=(send_next if up else send_prev).at[c, e, a],
            dst_ref=(from_prev if up else from_next).at[c, e, a],
            send_sem=u_send.at[int(up), index],
            recv_sem=u_recv.at[int(up), index],
            device_id={"energy": nxt_e if up else prv_e},
            device_id_type=MESH,
        )

    load_c.wait()

    def prepare(i, carry):
        mat = cbuf[i]
        high, low = split(mat)
        cleft[i, :, :orb] = high
        cleft[i, :, orb:] = low
        high, low = split(mat.T)
        for row in range(2):
            cright[i, row * orb : (row + 1) * orb, :orb] = high
            cright[i, row * orb : (row + 1) * orb, orb:] = low
        return carry

    lax.fori_loop(0, 2 * nbr, prepare, 0)
    load_g.wait()

    def turn(i, carry):
        c, e, a = i // 4, (i // 2) % 2, i % 2
        gt[c, e, a] = gbuf[c, e, 2 + a].T
        return carry

    lax.fori_loop(0, 8, turn, 0)

    first = ai * 2

    def fill(c, e):
        def body(b, carry):
            high, low = split(gbuf[c, e, b])
            for row in range(2):
                gs[b, row * orb : (row + 1) * orb, :orb] = high
                gs[b, row * orb : (row + 1) * orb, orb:] = low
            return carry

        lax.fori_loop(0, 6, body, 0)

    def products(a):
        for j in range(nbr):
            i = a * nbr + j
            near = jnp.clip(nbr_ref[i] - first + 2, 0, 5)
            both = jnp.dot(cleft[i], gs[near], preferred_element_type=F32)
            high, low = split(both[:, :orb] + both[:, orb:])
            inner = jnp.concatenate([high, low], axis=1)
            both = jnp.dot(inner, cright[i], preferred_element_type=F32)
            tbuf[j] = both[:, :orb] + both[:, orb:]

    def mix(a, targets):
        weights = [[ph_ref[(a * nbr + j) * 4 + k] for k in range(4)] for j in range(nbr)]
        rows = 32

        def body(r, carry):
            at = pl.ds(pl.multiple_of(r * rows, rows), rows)
            terms = [tbuf[j, at, :] for j in range(nbr)]
            for k in range(4):
                ref, add = targets[k]
                total = weights[0][k] * terms[0]
                for j in range(1, nbr):
                    total = total + weights[j][k] * terms[j]
                if add:
                    total = total + ref[at, :]
                ref[at, :] = total
            return carry

        lax.fori_loop(0, orb // rows, body, 0)

    def one_c(c, carry):
        for e in range(2):
            atom_copy(c, e, True).wait_recv()
            atom_copy(c, e, False).wait_recv()
            fill(c, e)

            def one_a(a, inner_carry):
                products(a)
                if e == 0:
                    mix(
                        a,
                        (
                            (send_next.at[c, 0, a], False),
                            (own.at[c, 1, a], False),
                            (send_prev.at[c, 1, a], False),
                            (send_prev.at[c, 0, a], False),
                        ),
                    )
                    energy_copy(c, 0, a, False).start()
                else:
                    mix(
                        a,
                        (
                            (send_next.at[c, 1, a], False),
                            (send_next.at[c, 0, a], True),
                            (own.at[c, 0, a], False),
                            (send_prev.at[c, 1, a], True),
                        ),
                    )
                    energy_copy(c, 0, a, True).start()
                    energy_copy(c, 1, a, True).start()
                    energy_copy(c, 1, a, False).start()
                return inner_carry

            lax.fori_loop(0, 2, one_a, 0)
        return carry

    lax.fori_loop(0, 2, one_c, 0)

    has_prev, has_next = ei > 0, ei < n_energy - 1
    rsrc[...] = jnp.zeros_like(rsrc)

    def out_copy(c, e, a):
        return pltpu.make_async_copy(
            own.at[c, e, a], sigma_out.at[c, e, a], o_sem.at[(c * 2 + e) * 2 + a]
        )

    for a in range(2):
        total = jnp.zeros((orb, orb), F32)
        for c in range(2):
            for e in range(2):
                energy_copy(c, e, a, True).wait_recv()
                energy_copy(c, e, a, False).wait_recv()
                block = own[c, e, a]
                block = block + jnp.where(has_prev, from_prev[c, e, a], 0.0)
                block = block + jnp.where(has_next, from_next[c, e, a], 0.0)
                own[c, e, a] = block
                term = block * gt[c, e, a]
                total = total + term if c == 0 else total - term
                out_copy(c, e, a).start()
        rsrc[a : a + 1, :] = jnp.sum(total.T, axis=0, keepdims=True)

    def rate_copy(sender, target):
        return pltpu.make_async_remote_copy(
            src_ref=rsrc,
            dst_ref=rslots.at[sender],
            send_sem=r_send.at[target],
            recv_sem=r_recv.at[sender],
            device_id={"energy": target},
            device_id_type=MESH,
        )

    def send_rate(p, carry):
        rate_copy(ei, lax.rem(ei + p, n_energy)).start()
        return carry

    lax.fori_loop(1, n_energy, send_rate, 0)
    rslots[ei] = rsrc[...]

    def wait_rate(p, carry):
        peer = lax.rem(ei + p, n_energy)
        rate_copy(peer, peer).wait_recv()
        return carry

    lax.fori_loop(1, n_energy, wait_rate, 0)
    total = rslots[0]
    for s in range(1, n_energy):
        total = total + rslots[s]
    rates_out[...] = total[:2] * (1.0 / (4.0 * 2 * n_energy))

    for c in range(2):
        for e in range(2):
            atom_copy(c, e, True).wait_send()
            atom_copy(c, e, False).wait_send()
            for a in range(2):
                energy_copy(c, e, a, True).wait_send()
                energy_copy(c, e, a, False).wait_send()
                out_copy(c, e, a).wait()

    def wait_rate_send(p, carry):
        rate_copy(ei, lax.rem(ei + p, n_energy)).wait_send()
        return carry

    lax.fori_loop(1, n_energy, wait_rate_send, 0)


def solution(mesh):
    n_energy, n_atom = mesh.shape["energy"], mesh.shape["atom"]

    def per_device(green, coupling, phonon, neighbours):
        orb, nbr = green.shape[-1], coupling.shape[1]
        rows = 2 * nbr
        whole = (2, 2, 2, orb, orb)
        any_space = pl.BlockSpec(memory_space=pl.ANY)
        smem = pl.BlockSpec(memory_space=pltpu.SMEM)
        sigma, rates = pl.pallas_call(
            functools.partial(kernel, n_energy, n_atom, nbr, orb),
            out_shape=(
                jax.ShapeDtypeStruct(whole, F32),
                jax.ShapeDtypeStruct((2, orb), F32),
            ),
            in_specs=[smem, smem, any_space, any_space],
            out_specs=(any_space, pl.BlockSpec(memory_space=pltpu.VMEM)),
            scratch_shapes=[
                pltpu.VMEM((2, 2, 6, orb, orb), F32),
                pltpu.VMEM((rows, orb, orb), F32),
                pltpu.VMEM((rows, orb, 2 * orb), BF16),
                pltpu.VMEM((rows, 2 * orb, 2 * orb), BF16),
                pltpu.VMEM((6, 2 * orb, 2 * orb), BF16),
                pltpu.VMEM((nbr, orb, orb), F32),
                pltpu.VMEM(whole, F32),
                pltpu.VMEM(whole, F32),
                pltpu.VMEM(whole, F32),
                pltpu.VMEM(whole, F32),
                pltpu.VMEM(whole, F32),
                pltpu.VMEM(whole, F32),
                pltpu.VMEM((8, orb), F32),
                pltpu.VMEM((n_energy, 8, orb), F32),
                pltpu.SemaphoreType.DMA((2,)),
                pltpu.SemaphoreType.DMA((2, 4)),
                pltpu.SemaphoreType.DMA((2, 4)),
                pltpu.SemaphoreType.DMA((2, 8)),
                pltpu.SemaphoreType.DMA((2, 8)),
                pltpu.SemaphoreType.DMA((n_energy,)),
                pltpu.SemaphoreType.DMA((n_energy,)),
                pltpu.SemaphoreType.DMA((8,)),
            ],
            compiler_params=pltpu.CompilerParams(collective_id=0, has_side_effects=True),
            name="self_energy",
        )(
            neighbours.reshape(rows),
            phonon.reshape(rows * 4),
            green,
            coupling.reshape(rows, orb, orb),
        )
        return sigma, rates

    return jax.shard_map(
        per_device,
        mesh=mesh,
        in_specs=(
            P(None, "energy", "atom", None, None),
            P("atom", None, None, None),
            P("atom", None, None),
            P("atom", None),
        ),
        out_specs=(P(None, "energy", "atom", None, None), P("atom", None)),
        check_vma=False,
    )
```

time: 223 us -> 78.3 us (0.35)
  the two profiles are of different devices: /device:TPU:246 before, /device:TPU:1 now
where the time goes in v1:
time: 78.3 us; the launch traced here: 78 us
  Pallas kernels  72.3 us (92%)
  local copies, waits for them, and re-layouts  5.08 us (6%)
    pallas_call x1, Pallas kernels, per_device(): pl.pallas_call(functools.partial(kernel, n_energy, n_atom, nbr, orb), out...  72.3 us
    unnamed x7, local copies, waits for them, and re-layouts  3.89 us

profile of v1, /device:TPU:1, one launch (start us, length us, event | category | flops | bytes accessed | tf_op | source)
XLA Modules:
  0.0 78.0 jit_solution(9671346138076853021)
XLA Ops:
  0.6 0.0 copy-start.1
  0.6 0.7 copy-done.1
  1.3 0.6 reshape.13.nbr_ref
  1.9 0.8 copy.7
  2.7 0.6 reshape.14.ph_ref
  3.3 72.3 %self_energy.1 = (f32[2,2,2,128,128]{4,3,2,1,0:T(8,128)}, f32[2,128]{1,0:T(2,128)}) custom-call(s32[12]{0:T(128)} %reshape.13.nbr_ref, f32[48]{0:T(128)} %reshape.14.ph_ref, f32[2,2,2,128,128]{4,3,2,1,0:T(8,128)} %green.1, f32[12,128,128]{2,1,0:T(8,128)} %bitcast.1), custom_call_target="tpu_custom_call" | custom-call | tf_op jit(solution)/shard_map/self_energy/pallas_call | solution.py:283
  75.6 0.0 copy-start
  75.6 1.9 %copy.10 = f32[2,2,2,128,128]{4,3,2,1,0:T(8,128)} copy(f32[2,2,2,128,128]{4,3,2,1,0:T(8,128)} %get-tuple-element.4) | data formatting | bytes 1048576
  77.5 0.0 copy-done
  77.5 0.6 copy.11
Async XLA Ops:
  0.6 0.7 copy-start.1
  75.6 1.9 %copy-start = (f32[2,128]{1,0:T(2,128)S(1)}, f32[2,128]{1,0:T(2,128)}, u32[]{:S(2)}) copy-start(f32[2,128]{1,0:T(2,128)} %get-tuple-element.5) | copy-start | bytes 3076

commit v2 on v1

--- a/solution.py
+++ b/solution.py
@@ -23,12 +23,14 @@
     n_atom,
     nbr,
     orb,
-    nbr_ref,
-    ph_ref,
+    nbr_hbm,
+    ph_hbm,
     green,
     coupling,
     sigma_out,
     rates_out,
+    nbr_ref,
+    ph_ref,
     gbuf,
     cbuf,
     cleft,
@@ -44,6 +46,8 @@
     rsrc,
     rslots,
     local_sem,
+    ready,
+    known,
     a_send,
     a_recv,
     u_send,
@@ -58,22 +62,19 @@
     nxt_e, prv_e = lax.rem(ei + 1, n_energy), lax.rem(ei + n_energy - 1, n_energy)
 
     barrier = pltpu.get_barrier_semaphore()
-    pl.semaphore_signal(barrier, inc=1, device_id={"atom": nxt_a}, device_id_type=MESH)
     pl.semaphore_signal(barrier, inc=1, device_id={"atom": prv_a}, device_id_type=MESH)
-
-    def greet(p, carry):
-        peer = lax.rem(ei + p, n_energy)
-        pl.semaphore_signal(barrier, inc=1, device_id={"energy": peer}, device_id_type=MESH)
-        return carry
-
-    lax.fori_loop(1, n_energy, greet, 0)
-
+    pl.semaphore_signal(barrier, inc=1, device_id={"energy": prv_e}, device_id_type=MESH)
+
+    load_n = pltpu.make_async_copy(nbr_hbm, nbr_ref, local_sem.at[2])
+    load_p = pltpu.make_async_copy(ph_hbm, ph_ref, local_sem.at[3])
     load_c = pltpu.make_async_copy(coupling, cbuf, local_sem.at[0])
     load_g = pltpu.make_async_copy(green, gbuf.at[:, :, pl.ds(2, 2)], local_sem.at[1])
+    load_n.start()
+    load_p.start()
     load_c.start()
     load_g.start()
 
-    pl.semaphore_wait(barrier, n_energy + 1)
+    not_last, not_first = ai < n_atom - 1, ai > 0
 
     def atom_copy(c, e, up):
         return pltpu.make_async_remote_copy(
@@ -85,10 +86,71 @@
             device_id_type=MESH,
         )
 
-    for c in range(2):
-        for e in range(2):
-            atom_copy(c, e, True).start()
-            atom_copy(c, e, False).start()
+    pl.semaphore_wait(barrier, 2)
+    pl.semaphore_signal(ready.at[0], inc=1, device_id={"atom": nxt_a}, device_id_type=MESH)
+    pl.semaphore_signal(ready.at[1], inc=1, device_id={"energy": nxt_e}, device_id_type=MESH)
+
+    @pl.when(not_last)
+    def _():
+        for c in range(2):
+            for e in range(2):
+                atom_copy(c, e, True).start()
+
+    load_c.wait()
+
+    def prepare(i, carry):
+        mat = cbuf[i]
+        high, low = split(mat)
+        cleft[i, :, :orb] = high
+        cleft[i, :, orb:] = low
+        high, low = split(mat.T)
+        for row in range(2):
+            cright[i, row * orb : (row + 1) * orb, :orb] = high
+            cright[i, row * orb : (row + 1) * orb, orb:] = low
+        return carry
+
+    lax.fori_loop(0, 2 * nbr, prepare, 0)
+
+    pl.semaphore_wait(ready.at[0], 1)
+
+    @pl.when(not_first)
+    def _():
+        for c in range(2):
+            for e in range(2):
+                atom_copy(c, e, False).start()
+
+    pl.semaphore_wait(ready.at[1], 1)
+
+    def tell(r):
+        reach = 2**r
+        for side, peer in enumerate((ei + reach, ei + n_energy - reach)):
+            pl.semaphore_signal(
+                known.at[side, r],
+                inc=1,
+                device_id={"energy": lax.rem(peer, n_energy)},
+                device_id_type=MESH,
+            )
+
+    def hear(r):
+        pl.semaphore_wait(known.at[0, r], 1)
+        pl.semaphore_wait(known.at[1, r], 1)
+
+    rounds = (n_energy // 2 - 1).bit_length()
+    tell(0)
+    load_g.wait()
+
+    def turn(i, carry):
+        c, e, a = i // 4, (i // 2) % 2, i % 2
+        gt[c, e, a] = gbuf[c, e, 2 + a].T
+        return carry
+
+    lax.fori_loop(0, 8, turn, 0)
+    load_n.wait()
+    load_p.wait()
+    for r in range(1, rounds):
+        hear(r - 1)
+        tell(r)
+    hear(rounds - 1)
 
     def energy_copy(c, e, a, up):
         index = (c * 2 + e) * 2 + a
@@ -101,29 +163,6 @@
             device_id_type=MESH,
         )
 
-    load_c.wait()
-
-    def prepare(i, carry):
-        mat = cbuf[i]
-        high, low = split(mat)
-        cleft[i, :, :orb] = high
-        cleft[i, :, orb:] = low
-        high, low = split(mat.T)
-        for row in range(2):
-            cright[i, row * orb : (row + 1) * orb, :orb] = high
-            cright[i, row * orb : (row + 1) * orb, orb:] = low
-        return carry
-
-    lax.fori_loop(0, 2 * nbr, prepare, 0)
-    load_g.wait()
-
-    def turn(i, carry):
-        c, e, a = i // 4, (i // 2) % 2, i % 2
-        gt[c, e, a] = gbuf[c, e, 2 + a].T
-        return carry
-
-    lax.fori_loop(0, 8, turn, 0)
-
     first = ai * 2
 
     def fill(c, e):
@@ -139,7 +178,7 @@
     def products(a):
         for j in range(nbr):
             i = a * nbr + j
-            near = jnp.clip(nbr_ref[i] - first + 2, 0, 5)
+            near = jnp.clip(nbr_ref[a, j] - first + 2, 0, 5)
             both = jnp.dot(cleft[i], gs[near], preferred_element_type=F32)
             high, low = split(both[:, :orb] + both[:, orb:])
             inner = jnp.concatenate([high, low], axis=1)
@@ -147,7 +186,7 @@
             tbuf[j] = both[:, :orb] + both[:, orb:]
 
     def mix(a, targets):
-        weights = [[ph_ref[(a * nbr + j) * 4 + k] for k in range(4)] for j in range(nbr)]
+        weights = [[ph_ref[a, k, j] for k in range(4)] for j in range(nbr)]
         rows = 32
 
         def body(r, carry):
@@ -167,8 +206,14 @@
 
     def one_c(c, carry):
         for e in range(2):
-            atom_copy(c, e, True).wait_recv()
-            atom_copy(c, e, False).wait_recv()
+            @pl.when(not_first)
+            def _():
+                atom_copy(c, e, True).wait_recv()
+
+            @pl.when(not_last)
+            def _():
+                atom_copy(c, e, False).wait_recv()
+
             fill(c, e)
 
             def one_a(a, inner_carry):
@@ -257,8 +302,14 @@
 
     for c in range(2):
         for e in range(2):
-            atom_copy(c, e, True).wait_send()
-            atom_copy(c, e, False).wait_send()
+            @pl.when(not_last)
+            def _():
+                atom_copy(c, e, True).wait_send()
+
+            @pl.when(not_first)
+            def _():
+                atom_copy(c, e, False).wait_send()
+
             for a in range(2):
                 energy_copy(c, e, a, True).wait_send()
                 energy_copy(c, e, a, False).wait_send()
@@ -279,16 +330,17 @@
         rows = 2 * nbr
         whole = (2, 2, 2, orb, orb)
         any_space = pl.BlockSpec(memory_space=pl.ANY)
-        smem = pl.BlockSpec(memory_space=pltpu.SMEM)
         sigma, rates = pl.pallas_call(
             functools.partial(kernel, n_energy, n_atom, nbr, orb),
             out_shape=(
                 jax.ShapeDtypeStruct(whole, F32),
                 jax.ShapeDtypeStruct((2, orb), F32),
             ),
-            in_specs=[smem, smem, any_space, any_space],
+            in_specs=[any_space] * 4,
             out_specs=(any_space, pl.BlockSpec(memory_space=pltpu.VMEM)),
             scratch_shapes=[
+                pltpu.SMEM((2, nbr), jnp.int32),
+                pltpu.SMEM((2, 4, nbr), F32),
                 pltpu.VMEM((2, 2, 6, orb, orb), F32),
                 pltpu.VMEM((rows, orb, orb), F32),
                 pltpu.VMEM((rows, orb, 2 * orb), BF16),
@@ -303,7 +355,9 @@
                 pltpu.VMEM(whole, F32),
                 pltpu.VMEM((8, orb), F32),
                 pltpu.VMEM((n_energy, 8, orb), F32),
-                pltpu.SemaphoreType.DMA((2,)),
+                pltpu.SemaphoreType.DMA((4,)),
+                pltpu.SemaphoreType.REGULAR((2,)),
+                pltpu.SemaphoreType.REGULAR((2, 8)),
                 pltpu.SemaphoreType.DMA((2, 4)),
                 pltpu.SemaphoreType.DMA((2, 4)),
                 pltpu.SemaphoreType.DMA((2, 8)),
@@ -315,8 +369,8 @@
             compiler_params=pltpu.CompilerParams(collective_id=0, has_side_effects=True),
             name="self_energy",
         )(
-            neighbours.reshape(rows),
-            phonon.reshape(rows * 4),
+            neighbours,
+            jnp.transpose(phonon, (0, 2, 1)),
             green,
             coupling.reshape(rows, orb, orb),
         )

time: 78.3 us -> 72.2 us (0.922)
  Pallas kernels: 72.3 us -> 68.4 us
  local copies, waits for them, and re-layouts: 5.08 us -> 2.44 us
    pallas_call x1, Pallas kernels: 72.3 us -> 68.4 us  [per_device(): pl.pallas_call(functools.partial(kernel, n_energy, n_atom, nbr, orb), out...]
    unnamed x7 -> x4, local copies, waits for them, and re-layouts: 3.89 us -> 2.44 us
    reshape x2 -> x0, local copies, waits for them, and re-layouts: 1.19 us -> none  [the longest x1 0.6 us: per_device(): phonon.reshape(rows * 4)]
where the time goes in v2:
time: 72.2 us; the launch traced here: 71.4 us
  Pallas kernels  68.4 us (95%)
  local copies, waits for them, and re-layouts  2.44 us (3%)
    pallas_call x1, Pallas kernels, per_device(): pl.pallas_call(functools.partial(kernel, n_energy, n_atom, nbr, orb), out...  68.4 us
    unnamed x4, local copies, waits for them, and re-layouts  2.44 us

profile of v2, /device:TPU:1, one launch (start us, length us, event | category | flops | bytes accessed | tf_op | source)
XLA Modules:
  0.0 71.4 jit_solution(16820931896461222187)
XLA Ops:
  0.6 68.4 %self_energy.1 = (f32[2,2,2,128,128]{4,3,2,1,0:T(8,128)}, f32[2,128]{1,0:T(2,128)}) custom-call(s32[2,6]{1,0:T(2,128)} %nbr_hbm.1, f32[2,4,6]{2,1,0:T(4,128)} %bitcast.3, f32[2,2,2,128,128]{4,3,2,1,0:T(8,128)} %green.1, f32[12,128,128]{2,1,0:T(8,128)} %bitcast.2), custom_call_target="tpu_custom_call" | custom-call | tf_op jit(solution)/shard_map/self_energy/pallas_call | solution.py:333
  69.0 0.0 copy-start
  69.0 1.9 %copy.8 = f32[2,2,2,128,128]{4,3,2,1,0:T(8,128)} copy(f32[2,2,2,128,128]{4,3,2,1,0:T(8,128)} %get-tuple-element.4) | data formatting | bytes 1048576
  70.9 0.0 copy-done
  70.9 0.6 copy.9
Async XLA Ops:
  69.0 1.9 %copy-start = (f32[2,128]{1,0:T(2,128)S(1)}, f32[2,128]{1,0:T(2,128)}, u32[]{:S(2)}) copy-start(f32[2,128]{1,0:T(2,128)} %get-tuple-element.5) | copy-start | bytes 3076

commit v3 on v2

--- a/solution.py
+++ b/solution.py
@@ -10,6 +10,7 @@
 MESH = pl.DeviceIdType.MESH
 F32 = jnp.float32
 BF16 = jnp.bfloat16
+Z_GROUPS = 4
 
 
 def split(x):
@@ -61,9 +62,22 @@
     nxt_a, prv_a = lax.rem(ai + 1, n_atom), lax.rem(ai + n_atom - 1, n_atom)
     nxt_e, prv_e = lax.rem(ei + 1, n_energy), lax.rem(ei + n_energy - 1, n_energy)
 
+    group = lax.rem(ai, Z_GROUPS)
+    first_group, last_group = group == 0, group == Z_GROUPS - 1
     barrier = pltpu.get_barrier_semaphore()
-    pl.semaphore_signal(barrier, inc=1, device_id={"atom": prv_a}, device_id_type=MESH)
-    pl.semaphore_signal(barrier, inc=1, device_id={"energy": prv_e}, device_id_type=MESH)
+
+    def greet(sem, axis, peer):
+        pl.semaphore_signal(sem, inc=1, device_id={axis: peer}, device_id_type=MESH)
+
+    greet(barrier, "energy", prv_e)
+
+    @pl.when(jnp.logical_not(last_group))
+    def _():
+        greet(barrier, "atom", nxt_a)
+
+    @pl.when(first_group)
+    def _():
+        greet(barrier, "atom", prv_a)
 
     load_n = pltpu.make_async_copy(nbr_hbm, nbr_ref, local_sem.at[2])
     load_p = pltpu.make_async_copy(ph_hbm, ph_ref, local_sem.at[3])
@@ -86,15 +100,45 @@
             device_id_type=MESH,
         )
 
-    pl.semaphore_wait(barrier, 2)
-    pl.semaphore_signal(ready.at[0], inc=1, device_id={"atom": nxt_a}, device_id_type=MESH)
-    pl.semaphore_signal(ready.at[1], inc=1, device_id={"energy": nxt_e}, device_id_type=MESH)
-
-    @pl.when(not_last)
-    def _():
+    def send_up():
+        @pl.when(not_last)
+        def _():
+            for c in range(2):
+                for e in range(2):
+                    atom_copy(c, e, True).start()
+
+    def send_down(c, e):
+        @pl.when(not_first)
+        def _():
+            atom_copy(c, e, False).start()
+
+    @pl.when(first_group)
+    def _():
+        pl.semaphore_wait(barrier, 1)
+
+    @pl.when(jnp.logical_and(jnp.logical_not(first_group), jnp.logical_not(last_group)))
+    def _():
+        pl.semaphore_wait(barrier, 2)
+
+    @pl.when(last_group)
+    def _():
+        pl.semaphore_wait(barrier, 3)
+        greet(ready.at[0], "atom", nxt_a)
+        send_up()
+
+    greet(ready.at[2], "energy", nxt_e)
+
+    @pl.when(jnp.logical_not(first_group))
+    def _():
+        greet(ready.at[1], "atom", prv_a)
         for c in range(2):
             for e in range(2):
-                atom_copy(c, e, True).start()
+                send_down(c, e)
+
+    @pl.when(first_group)
+    def _():
+        pl.semaphore_wait(ready.at[1], 1)
+        send_up()
 
     load_c.wait()
 
@@ -111,15 +155,19 @@
 
     lax.fori_loop(0, 2 * nbr, prepare, 0)
 
-    pl.semaphore_wait(ready.at[0], 1)
-
-    @pl.when(not_first)
-    def _():
+    @pl.when(jnp.logical_and(jnp.logical_not(first_group), jnp.logical_not(last_group)))
+    def _():
+        pl.semaphore_wait(ready.at[1], 1)
+        send_up()
+
+    @pl.when(first_group)
+    def _():
+        pl.semaphore_wait(ready.at[0], 1)
         for c in range(2):
             for e in range(2):
-                atom_copy(c, e, False).start()
-
-    pl.semaphore_wait(ready.at[1], 1)
+                send_down(c, e)
+
+    pl.semaphore_wait(ready.at[2], 1)
 
     def tell(r):
         reach = 2**r
@@ -245,6 +293,7 @@
                 return inner_carry
 
             lax.fori_loop(0, 2, one_a, 0)
+
         return carry
 
     lax.fori_loop(0, 2, one_c, 0)
@@ -356,7 +405,7 @@
                 pltpu.VMEM((8, orb), F32),
                 pltpu.VMEM((n_energy, 8, orb), F32),
                 pltpu.SemaphoreType.DMA((4,)),
-                pltpu.SemaphoreType.REGULAR((2,)),
+                pltpu.SemaphoreType.REGULAR((3,)),
                 pltpu.SemaphoreType.REGULAR((2, 8)),
                 pltpu.SemaphoreType.DMA((2, 4)),
                 pltpu.SemaphoreType.DMA((2, 4)),
@@ -366,13 +415,18 @@
                 pltpu.SemaphoreType.DMA((n_energy,)),
                 pltpu.SemaphoreType.DMA((8,)),
             ],
-            compiler_params=pltpu.CompilerParams(collective_id=0, has_side_effects=True),
+            compiler_params=pltpu.CompilerParams(collective_id=0, has_side_effects=True, vmem_limit_bytes=14 * 2**20),
             name="self_energy",
         )(
-            neighbours,
-            jnp.transpose(phonon, (0, 2, 1)),
-            green,
-            coupling.reshape(rows, orb, orb),
+            *(
+                pltpu.with_memory_space_constraint(x, pltpu.HBM)
+                for x in (
+                    neighbours,
+                    jnp.transpose(phonon, (0, 2, 1)),
+                    green,
+                    coupling.reshape(rows, orb, orb),
+                )
+            )
         )
         return sigma, rates
 

time: 72.2 us -> 71.1 us (0.985)
  local copies, waits for them, and re-layouts: 2.44 us -> 1.36 us
    unnamed x4 -> x2, local copies, waits for them, and re-layouts: 2.44 us -> 1.36 us
where the time goes in v3:
time: 71.1 us; the launch traced here: 70.9 us
  Pallas kernels  68.9 us (97%)
  local copies, waits for them, and re-layouts  1.36 us (2%)
    pallas_call x1, Pallas kernels, per_device(): pl.pallas_call(functools.partial(kernel, n_energy, n_atom, nbr, orb), out...  68.9 us

profile of v3, /device:TPU:1, one launch (start us, length us, event | category | flops | bytes accessed | tf_op | source)
XLA Modules:
  0.0 70.9 jit_solution(311463545764843113)
XLA Ops:
  0.6 68.9 %self_energy.1 = (f32[2,2,2,128,128]{4,3,2,1,0:T(8,128)S(1)}, f32[2,128]{1,0:T(2,128)S(1)}) custom-call(s32[2,6]{1,0:T(2,128)} %nbr_hbm.1, f32[2,4,6]{2,1,0:T(4,128)} %bitcast.3, f32[2,2,2,128,128]{4,3,2,1,0:T(8,128)} %green.1, f32[12,128,128]{2,1,0:T(8,128)} %bitcast.2), custom_call_target="tpu_custom_call" | custom-call | tf_op jit(solution)/shard_map/self_energy/pallas_call | solution.py:382
  69.6 0.8 %copy.8 = f32[2,2,2,128,128]{4,3,2,1,0:T(8,128)} copy(f32[2,2,2,128,128]{4,3,2,1,0:T(8,128)S(1)} %get-tuple-element.4) | data formatting | bytes 1048576
  70.4 0.6 copy.9

commit v4 on v3

--- a/solution.py
+++ b/solution.py
@@ -299,7 +299,6 @@
     lax.fori_loop(0, 2, one_c, 0)
 
     has_prev, has_next = ei > 0, ei < n_energy - 1
-    rsrc[...] = jnp.zeros_like(rsrc)
 
     def out_copy(c, e, a):
         return pltpu.make_async_copy(
@@ -338,17 +337,6 @@
     lax.fori_loop(1, n_energy, send_rate, 0)
     rslots[ei] = rsrc[...]
 
-    def wait_rate(p, carry):
-        peer = lax.rem(ei + p, n_energy)
-        rate_copy(peer, peer).wait_recv()
-        return carry
-
-    lax.fori_loop(1, n_energy, wait_rate, 0)
-    total = rslots[0]
-    for s in range(1, n_energy):
-        total = total + rslots[s]
-    rates_out[...] = total[:2] * (1.0 / (4.0 * 2 * n_energy))
-
     for c in range(2):
         for e in range(2):
             @pl.when(not_last)
@@ -369,6 +357,17 @@
         return carry
 
     lax.fori_loop(1, n_energy, wait_rate_send, 0)
+
+    def wait_rate(p, carry):
+        peer = lax.rem(ei + p, n_energy)
+        rate_copy(peer, peer).wait_recv()
+        return carry
+
+    lax.fori_loop(1, n_energy, wait_rate, 0)
+    total = rslots[0]
+    for s in range(1, n_energy):
+        total = total + rslots[s]
+    rates_out[...] = total * (1.0 / (4.0 * 2 * n_energy))
 
 
 def solution(mesh):
@@ -402,8 +401,8 @@
                 pltpu.VMEM(whole, F32),
                 pltpu.VMEM(whole, F32),
                 pltpu.VMEM(whole, F32),
-                pltpu.VMEM((8, orb), F32),
-                pltpu.VMEM((n_energy, 8, orb), F32),
+                pltpu.VMEM((2, orb), F32),
+                pltpu.VMEM((n_energy, 2, orb), F32),
                 pltpu.SemaphoreType.DMA((4,)),
                 pltpu.SemaphoreType.REGULAR((3,)),
                 pltpu.SemaphoreType.REGULAR((2, 8)),

time: 71.1 us -> 70.3 us (0.989)
    pallas_call x1, Pallas kernels: 68.9 us -> 68.2 us  [per_device(): pl.pallas_call(functools.partial(kernel, n_energy, n_atom, nbr, orb), out...]
where the time goes in v4:
time: 70.3 us; the launch traced here: 70.2 us
  Pallas kernels  68.2 us (97%)
  local copies, waits for them, and re-layouts  1.36 us (2%)
    pallas_call x1, Pallas kernels, per_device(): pl.pallas_call(functools.partial(kernel, n_energy, n_atom, nbr, orb), out...  68.2 us

profile of v4, /device:TPU:1, one launch (start us, length us, event | category | flops | bytes accessed | tf_op | source)
XLA Modules:
  0.0 70.2 jit_solution(12064904974642866449)
XLA Ops:
  0.6 68.2 %self_energy.1 = (f32[2,2,2,128,128]{4,3,2,1,0:T(8,128)S(1)}, f32[2,128]{1,0:T(2,128)S(1)}) custom-call(s32[2,6]{1,0:T(2,128)} %nbr_hbm.1, f32[2,4,6]{2,1,0:T(4,128)} %bitcast.3, f32[2,2,2,128,128]{4,3,2,1,0:T(8,128)} %green.1, f32[12,128,128]{2,1,0:T(8,128)} %bitcast.2), custom_call_target="tpu_custom_call" | custom-call | tf_op jit(solution)/shard_map/self_energy/pallas_call | solution.py:381
  68.8 0.8 %copy.8 = f32[2,2,2,128,128]{4,3,2,1,0:T(8,128)} copy(f32[2,2,2,128,128]{4,3,2,1,0:T(8,128)S(1)} %get-tuple-element.4) | data formatting | bytes 1048576
  69.6 0.6 copy.9

commit v5 on v4

--- a/solution.py
+++ b/solution.py
@@ -100,12 +100,21 @@
             device_id_type=MESH,
         )
 
+    def send_up_last():
+        @pl.when(not_last)
+        def _():
+            atom_copy(1, 1, True).start()
+
     def send_up():
         @pl.when(not_last)
         def _():
-            for c in range(2):
-                for e in range(2):
-                    atom_copy(c, e, True).start()
+            atom_copy(0, 0, True).start()
+            atom_copy(0, 1, True).start()
+            atom_copy(1, 0, True).start()
+
+        @pl.when(not_first)
+        def _():
+            send_up_last()
 
     def send_down(c, e):
         @pl.when(not_first)
@@ -163,9 +172,9 @@
     @pl.when(first_group)
     def _():
         pl.semaphore_wait(ready.at[0], 1)
-        for c in range(2):
-            for e in range(2):
-                send_down(c, e)
+        send_down(0, 0)
+        send_down(0, 1)
+        send_down(1, 0)
 
     pl.semaphore_wait(ready.at[2], 1)
 
@@ -293,10 +302,18 @@
                 return inner_carry
 
             lax.fori_loop(0, 2, one_a, 0)
+            if e == 1:
+                @pl.when(jnp.logical_and(c == 0, jnp.logical_not(not_first)))
+                def _():
+                    send_up_last()
 
         return carry
 
     lax.fori_loop(0, 2, one_c, 0)
+
+    @pl.when(first_group)
+    def _():
+        send_down(1, 1)
 
     has_prev, has_next = ei > 0, ei < n_energy - 1
 

time: 70.3 us -> 71.4 us (1.016)
  Pallas kernels: 68.2 us -> 69.3 us
    pallas_call x1, Pallas kernels: 68.2 us -> 69.3 us  [per_device(): pl.pallas_call(functools.partial(kernel, n_energy, n_atom, nbr, orb), out...]
where the time goes in v5:
time: 71.4 us; the launch traced here: 71.3 us
  Pallas kernels  69.3 us (97%)
  local copies, waits for them, and re-layouts  1.36 us (2%)
    pallas_call x1, Pallas kernels, per_device(): pl.pallas_call(functools.partial(kernel, n_energy, n_atom, nbr, orb), out...  69.3 us

profile of v5, /device:TPU:1, one launch (start us, length us, event | category | flops | bytes accessed | tf_op | source)
XLA Modules:
  0.0 71.3 jit_solution(12552997154964562737)
XLA Ops:
  0.6 69.3 %self_energy.1 = (f32[2,2,2,128,128]{4,3,2,1,0:T(8,128)S(1)}, f32[2,128]{1,0:T(2,128)S(1)}) custom-call(s32[2,6]{1,0:T(2,128)} %nbr_hbm.1, f32[2,4,6]{2,1,0:T(4,128)} %bitcast.3, f32[2,2,2,128,128]{4,3,2,1,0:T(8,128)} %green.1, f32[12,128,128]{2,1,0:T(8,128)} %bitcast.2), custom_call_target="tpu_custom_call" | custom-call | tf_op jit(solution)/shard_map/self_energy/pallas_call | solution.py:398
  69.9 0.8 %copy.8 = f32[2,2,2,128,128]{4,3,2,1,0:T(8,128)} copy(f32[2,2,2,128,128]{4,3,2,1,0:T(8,128)S(1)} %get-tuple-element.4) | data formatting | bytes 1048576
  70.7 0.6 copy.9

commit v6 on v4

--- a/solution.py
+++ b/solution.py
@@ -75,7 +75,7 @@
     def _():
         greet(barrier, "atom", nxt_a)
 
-    @pl.when(first_group)
+    @pl.when(jnp.logical_or(first_group, group == 1))
     def _():
         greet(barrier, "atom", prv_a)
 
@@ -112,11 +112,7 @@
         def _():
             atom_copy(c, e, False).start()
 
-    @pl.when(first_group)
-    def _():
-        pl.semaphore_wait(barrier, 1)
-
-    @pl.when(jnp.logical_and(jnp.logical_not(first_group), jnp.logical_not(last_group)))
+    @pl.when(jnp.logical_not(last_group))
     def _():
         pl.semaphore_wait(barrier, 2)
 
@@ -130,14 +126,16 @@
 
     @pl.when(jnp.logical_not(first_group))
     def _():
-        greet(ready.at[1], "atom", prv_a)
+        @pl.when(group > 1)
+        def _():
+            greet(ready.at[1], "atom", prv_a)
+
         for c in range(2):
             for e in range(2):
                 send_down(c, e)
 
     @pl.when(first_group)
     def _():
-        pl.semaphore_wait(ready.at[1], 1)
         send_up()
 
     load_c.wait()
@@ -163,9 +161,9 @@
     @pl.when(first_group)
     def _():
         pl.semaphore_wait(ready.at[0], 1)
-        for c in range(2):
-            for e in range(2):
-                send_down(c, e)
+        send_down(0, 0)
+        send_down(0, 1)
+        send_down(1, 0)
 
     pl.semaphore_wait(ready.at[2], 1)
 
@@ -298,6 +296,10 @@
 
     lax.fori_loop(0, 2, one_c, 0)
 
+    @pl.when(first_group)
+    def _():
+        send_down(1, 1)
+
     has_prev, has_next = ei > 0, ei < n_energy - 1
 
     def out_copy(c, e, a):

time: 70.3 us -> 69.4 us (0.987)
  the two profiles are of different devices: /device:TPU:1 before, /device:TPU:57 now
where the time goes in v6:
time: 69.4 us; the launch traced here: 69.2 us
  Pallas kernels  67.2 us (97%)
  local copies, waits for them, and re-layouts  1.36 us (2%)
    pallas_call x1, Pallas kernels, per_device(): pl.pallas_call(functools.partial(kernel, n_energy, n_atom, nbr, orb), out...  67.2 us

profile of v6, /device:TPU:57, one launch (start us, length us, event | category | flops | bytes accessed | tf_op | source)
XLA Modules:
  0.0 69.2 jit_solution(982218678038677311)
XLA Ops:
  0.6 67.2 %self_energy.1 = (f32[2,2,2,128,128]{4,3,2,1,0:T(8,128)S(1)}, f32[2,128]{1,0:T(2,128)S(1)}) custom-call(s32[2,6]{1,0:T(2,128)} %nbr_hbm.1, f32[2,4,6]{2,1,0:T(4,128)} %bitcast.3, f32[2,2,2,128,128]{4,3,2,1,0:T(8,128)} %green.1, f32[12,128,128]{2,1,0:T(8,128)} %bitcast.2), custom_call_target="tpu_custom_call" | custom-call | tf_op jit(solution)/shard_map/self_energy/pallas_call | solution.py:383
  67.9 0.8 %copy.8 = f32[2,2,2,128,128]{4,3,2,1,0:T(8,128)} copy(f32[2,2,2,128,128]{4,3,2,1,0:T(8,128)S(1)} %get-tuple-element.4) | data formatting | bytes 1048576
  68.7 0.6 copy.9
